TPU v7x, 32 devices: a whole 2x2x4 slice. The times are simulated.
32 devices in a mesh: seq: 8 (over z, x), tp: 4 (over y, core).
Axes of the slice: x: 2, y: 2, z: 4, core: 2. Of those that a mesh axis runs over, the one named last changes fastest.
Arguments:
- tokens: bfloat16 [2048, 1536], P('seq'), may hold values from -6 to 6
- norm1_gain: bfloat16 [1536], replicated, may hold values from 0.25 to 1.75
- w_query: bfloat16 [1536, 1536], P('tp'), may hold values from -0.15625 to 0.15625
- key_weight: bfloat16 [512, 1536], P('tp'), may hold values from -0.4375 to 0.4375
- value_weight: bfloat16 [512, 1536], P('tp'), may hold values from -0.15625 to 0.15625
- rotated_key_cache: bfloat16 [4, 8, 524288], P(None, 'tp', 'seq'), may hold values from -60 to 60
- stored_value_cache: bfloat16 [4, 8, 524288], P(None, 'tp', 'seq'), may hold values from -6 to 6
- cache_len: int32 [4], replicated, may hold values from 1 to 8192, 16384 in all
- w_out: bfloat16 [1536, 1536], P('tp'), may hold values from -0.15625 to 0.15625
- norm2_gain: bfloat16 [1536], replicated, may hold values from 0.25 to 1.75
- w_router: bfloat16 [1536, 40], replicated, may hold values from -0.0546875 to 0.0546875
- expert_ids: int32 [2048, 8], P('seq'), may hold values from 0 to 39, all different within a row
- w_gate_up: bfloat16 [40, 2, 1536, 512], P('tp', None, 'seq'), may hold values from -0.15625 to 0.15625
- w_down: bfloat16 [40, 512, 1536], P('tp', 'seq'), may hold values from -0.5 to 0.5
Outputs:
- attn_out: bfloat16 [2048, 1536], P('seq')
- expert_out: bfloat16 [2048, 1536], P('seq')
Inputs may be any that keep to these rules, and one draw needn't show every extreme that they name: `cache_len`: request lengths of 1 to 8192; one request fills all 8192 positions. `expert_ids`: each row names 8 different experts; every expert is named.
All inputs are finite; a program needn't handle non-finite values.
Results may differ from a plain program's by a relative error of at most 0.03.
Values may be sent and summed in bfloat16 or wider, within the bound.
A program may use at most 192 MiB of HBM per device.

v0:
```python
import jax
import jax.numpy as jnp
from jax import lax
from jax.sharding import PartitionSpec as P

HEAD_SIZE = 64
FRESH_TOKENS = 512
EPS = 1e-05
THETA = 10000.0
NEGATIVE = -1e30


def combined_all(x, axis, join):
    gathered = jax.tree.map(
        lambda a, kind: lax.all_gather(a.astype(kind), axis),
        x,
        (jnp.bfloat16, jnp.bfloat16, jnp.bfloat16),
    )

    def take(source):
        return jax.tree.map(
            lambda a, own: lax.dynamic_index_in_dim(a, source, 0, False).astype(own.dtype),
            gathered,
            x,
        )

    return lax.fori_loop(
        1, lax.axis_size(axis), lambda source, state: join(state, take(source)), take(0)
    )


def rms_norm(values, gain):
    mean_square = jnp.mean(values * values, axis=-1, keepdims=True)
    return values * lax.rsqrt(mean_square + EPS) * gain.astype(values.dtype)


def apply_rotary(values, positions):
    half_dim = values.shape[-1] // 2
    exponent = jnp.arange(half_dim, dtype=jnp.float32) * (2.0 / values.shape[-1])
    freqs = THETA ** (-exponent)
    angles = positions[:, None] * freqs[None, :]
    cosine = jnp.cos(angles)[:, None, :]
    sine = jnp.sin(angles)[:, None, :]
    first = values[..., :half_dim]
    second = values[..., half_dim:]
    return jnp.concatenate(
        [first * cosine - second * sine, second * cosine + first * sine], axis=-1
    )


def apply_projection(normalized_input, weight):
    return jnp.einsum("td,fd->tf", normalized_input, weight, preferred_element_type=jnp.float32)


def lookup(table, index):
    hits = index[:, None] == jnp.arange(table.shape[0], dtype=jnp.int32)[None, :]
    return jnp.sum(jnp.where(hits, table[None, :], 0), axis=1)


def join_parts(first, second):
    out_a, peak_a, sum_a = first
    out_b, peak_b, sum_b = second
    top = jnp.maximum(peak_a, peak_b)
    factor_a = jnp.exp(peak_a - top)
    factor_b = jnp.exp(peak_b - top)
    return (
        out_a * factor_a[..., None] + out_b * factor_b[..., None],
        top,
        sum_a * factor_a + sum_b * factor_b,
    )


def per_device(
    tokens,
    norm1_gain,
    w_query,
    key_weight,
    value_weight,
    rotated_key_cache,
    stored_value_cache,
    cache_len,
    w_out,
    norm2_gain,
    w_router,
    expert_ids,
    w_gate_up,
    w_down,
):
    tok_rows, width = tokens.shape
    seq_pos = lax.axis_index("seq")
    tp_pos = lax.axis_index("tp")
    local_q = w_query.shape[0] // HEAD_SIZE
    local_kv = key_weight.shape[0] // HEAD_SIZE
    query_group = local_q // local_kv
    requests = rotated_key_cache.shape[0]
    span = rotated_key_cache.shape[2] // HEAD_SIZE
    scale = HEAD_SIZE ** (-0.5)
    inputs = tokens.astype(jnp.float32)
    normalized_input = rms_norm(inputs, norm1_gain).astype(jnp.bfloat16)
    row_ids = seq_pos * tok_rows + jnp.arange(tok_rows, dtype=jnp.int32)
    owners = row_ids // FRESH_TOKENS
    positions = lookup(cache_len, owners) + row_ids % FRESH_TOKENS
    angle_position = positions.astype(jnp.float32)
    query_vector = apply_rotary(
        apply_projection(normalized_input, w_query).reshape(tok_rows, local_q, HEAD_SIZE),
        angle_position,
    ).astype(jnp.bfloat16)
    fresh_key = apply_rotary(
        apply_projection(normalized_input, key_weight).reshape(tok_rows, local_kv, HEAD_SIZE),
        angle_position,
    ).astype(jnp.bfloat16)
    fresh_value = (
        apply_projection(normalized_input, value_weight)
        .astype(jnp.bfloat16)
        .reshape(tok_rows, local_kv, HEAD_SIZE)
    )
    all_query = lax.all_gather(
        query_vector.reshape(tok_rows, local_q * HEAD_SIZE), "seq", axis=0, tiled=True
    )
    cache_pos = seq_pos * span + jnp.arange(span, dtype=jnp.int32)
    key_pos = jnp.concatenate([cache_pos, positions])

    def one_request(request_index):
        length = lax.dynamic_index_in_dim(cache_len, request_index, 0, keepdims=False)
        query_rows = lax.dynamic_slice_in_dim(
            all_query, request_index * FRESH_TOKENS, FRESH_TOKENS, 0
        ).reshape(FRESH_TOKENS, local_kv, query_group, HEAD_SIZE)
        query_pos = length + jnp.arange(FRESH_TOKENS, dtype=jnp.int32)
        prior_keys = jnp.transpose(
            lax.dynamic_index_in_dim(rotated_key_cache, request_index, 0, keepdims=False).reshape(
                local_kv, span, HEAD_SIZE
            ),
            (1, 0, 2),
        )
        prior_values = jnp.transpose(
            lax.dynamic_index_in_dim(stored_value_cache, request_index, 0, keepdims=False).reshape(
                local_kv, span, HEAD_SIZE
            ),
            (1, 0, 2),
        )
        keys = jnp.concatenate([prior_keys, fresh_key], axis=0)
        values = jnp.concatenate([prior_values, fresh_value], axis=0)
        usable = jnp.concatenate([cache_pos < length, owners == request_index])
        allowed = usable[None, :] & (key_pos[None, :] <= query_pos[:, None])
        scores = (
            jnp.einsum("nhgd,khd->hgnk", query_rows, keys, preferred_element_type=jnp.float32)
            * scale
        )
        scores = jnp.where(allowed[None, None], scores, NEGATIVE)
        peak = jnp.max(scores, axis=-1)
        weights = jnp.where(allowed[None, None], jnp.exp(scores - peak[..., None]), 0.0)
        total = jnp.sum(weights, axis=-1)
        mixed = jnp.einsum(
            "hgnk,khd->nhgd",
            weights.astype(jnp.bfloat16),
            values,
            preferred_element_type=jnp.float32,
        )
        return (
            mixed.reshape(FRESH_TOKENS, local_q, HEAD_SIZE),
            jnp.transpose(peak, (2, 0, 1)).reshape(FRESH_TOKENS, local_q),
            jnp.transpose(total, (2, 0, 1)).reshape(FRESH_TOKENS, local_q),
        )

    part_out, part_peak, part_sum = lax.map(one_request, jnp.arange(requests, dtype=jnp.int32))
    total_rows = requests * FRESH_TOKENS
    part_out = part_out.reshape(total_rows, local_q, HEAD_SIZE)
    part_peak = part_peak.reshape(total_rows, local_q)
    part_sum = part_sum.reshape(total_rows, local_q)
    full_out, full_peak, full_sum = combined_all((part_out, part_peak, part_sum), "seq", join_parts)
    own_out = lax.dynamic_slice_in_dim(full_out, seq_pos * tok_rows, tok_rows, 0)
    own_sum = lax.dynamic_slice_in_dim(full_sum, seq_pos * tok_rows, tok_rows, 0)
    heads_out = (
        (own_out / own_sum[..., None]).astype(jnp.bfloat16).reshape(tok_rows, local_q * HEAD_SIZE)
    )
    attn_part = jnp.dot(heads_out, w_out, preferred_element_type=jnp.float32)
    attn = lax.psum(attn_part.astype(jnp.bfloat16), "tp").astype(jnp.float32)
    attn_out = attn.astype(jnp.bfloat16)
    normed2 = rms_norm(inputs + attn, norm2_gain).astype(jnp.bfloat16)
    logits = jnp.dot(normed2, w_router, preferred_element_type=jnp.float32)
    experts_all = w_router.shape[1]
    picked_all = expert_ids[:, :, None] == jnp.arange(experts_all, dtype=jnp.int32)[None, None, :]
    chosen = jnp.sum(jnp.where(picked_all, logits[:, None, :], 0.0), axis=-1)
    gates = jax.nn.softmax(chosen, axis=-1)
    local_experts = w_gate_up.shape[0]
    local_ids = tp_pos * local_experts + jnp.arange(local_experts, dtype=jnp.int32)
    picked = expert_ids[:, :, None] == local_ids[None, None, :]
    share = jnp.sum(jnp.where(picked, gates[:, :, None], 0.0), axis=1)
    both = jnp.einsum(
        "td,ecdf->tecf",
        normed2,
        lax.all_gather(w_gate_up, "seq", axis=2, tiled=True),
        preferred_element_type=jnp.float32,
    )
    hidden = (jax.nn.silu(both[:, :, 0]) * both[:, :, 1] * share[:, :, None]).astype(jnp.bfloat16)
    moe_part = jnp.einsum(
        "tef,efd->td",
        hidden,
        lax.all_gather(w_down, "seq", axis=1, tiled=True),
        preferred_element_type=jnp.float32,
    )
    expert_out = lax.psum(moe_part.astype(jnp.bfloat16), "tp")
    return (attn_out, expert_out)


def solution(mesh):
    return jax.shard_map(
        per_device,
        mesh=mesh,
        in_specs=(
            P("seq", None),
            P(),
            P("tp", None),
            P("tp", None),
            P("tp", None),
            P(None, "tp", "seq"),
            P(None, "tp", "seq"),
            P(),
            P("tp", None),
            P(),
            P(),
            P("seq", None),
            P("tp", None, "seq", None),
            P("tp", "seq", None),
        ),
        out_specs=(P("seq", None), P("seq", None)),
        check_vma=False,
    )
```

profile of v0, /device:TPU:0, one launch (start us, length us, event | category | flops | bytes accessed | tf_op | source)
XLA Modules:
  0.0 1429.9 jit_solution(5135392663269853709)
XLA Ops:
  15.7 45.8 %all-gather.5.cloned.1.call-done = bf16[2048,384]{0,1:T(8,128)(2,1)} async-done(((bf16[256,384]{0,1:T(8,128)(2,1)}), bf16[2048,384]{0,1:T(8,128)(2,1)}) %all-gather.5.cloned.1.call-update) | async-done | bytes 1572880 | tf_op jit(solution)/shard_map/all_gather | solution.py:117
  61.5 112.0 %while.35 = (s32[]{:T(128)}, bf16[4,512,6,64]{1,3,2,0:T(8,128)(2,1)}, bf16[4,512,6]{1,2,0:T(8,128)(2,1)S(1)}, bf16[4,512,6]{1,2,0:T(8,128)(2,1)S(1)}, s32[4]{0:T...) while((s32[]{:T(128)}, ...), condition=%wide.region_5.6_spmd.clone, body=%wide.region_2.5_spmd.clone.sunk | while | flops 1060374528 | bytes 119003984 | solution.py:165
  80.9 7.9 fusion.78
  108.8 7.9 fusion.78
  136.9 7.9 fusion.78
  164.9 7.9 fusion.78
  178.6 31.7 %all_gather.23 = bf16[8,2048,6]{1,2,0:T(8,128)(2,1)S(1)} all-gather(bf16[1,2048,6]{1,2,0:T(8,128)(2,1)S(1)} %bitcast.154), channel_id=1, replica_groups=mesh['seq'=8,'tp'=4] {'seq'}, dimensions={0}, use_global_device_ids=true | all-gather | bytes 221184 | tf_op jit(solution)/shard_map/all_gather | solution.py:15
  211.8 32.3 %all_gather.24 = bf16[8,2048,6]{1,2,0:T(8,128)(2,1)S(1)} all-gather(bf16[1,2048,6]{1,2,0:T(8,128)(2,1)S(1)} %bitcast.155), channel_id=1, replica_groups=mesh['seq'=8,'tp'=4] {'seq'}, dimensions={0}, use_global_device_ids=true | all-gather | bytes 221184 | tf_op jit(solution)/shard_map/all_gather | solution.py:15
  244.4 112.8 %all-gather.7.cloned.1.call-done = bf16[8,2048,6,64]{1,3,2,0:T(8,128)(2,1)} async-done(((bf16[1,2048,6,64]{1,3,2,0:T(8,128)(2,1)}), bf16[8,2048,6,64]{1,3,2,0:T(8,128)(2,1)}) %all-gather.7.cloned.1.call-update) | async-done | bytes 12582928 | tf_op jit(solution)/shard_map/all_gather | solution.py:15
  360.7 6.6 copy.80
  367.3 147.2 %while.34 = (s32[]{:T(128)}, f32[2048,6,64]{2,1,0:T(8,128)}, f32[2048,6]{1,0:T(8,128)}, f32[2048,6]{1,0:T(8,128)S(1)}, bf16[8,2048,6]{1,2,0:T(8,128)(2,1)S(1)}, ...) while((s32[]{:T(128)}, f32[2048,6,64]{2,1,0:T(8,128)}, ...), condition=%wide.region_7.8_spmd, body=%wide.region_6.7_spmd.sunk | while | flops 3244037 | bytes 18334016 | solution.py:27
  374.3 4.2 copy.103
  378.6 9.7 fusion.73
  395.3 4.2 copy.103
  399.6 9.7 fusion.73
  416.4 4.2 copy.103
  420.6 9.7 fusion.73
  437.4 4.2 copy.103
  441.7 9.7 fusion.73
  458.4 4.2 copy.103
  462.7 9.7 fusion.73
  479.5 4.2 copy.103
  483.7 9.7 fusion.73
  500.5 4.2 copy.103
  504.8 9.7 fusion.73
  514.5 6.3 copy.86
  524.8 31.7 %all-reduce.3.cloned.1.call-done = bf16[256,1536]{1,0:T(8,128)(2,1)} async-done(((bf16[256,1536]{1,0:T(8,128)(2,1)}), bf16[256,1536]{1,0:T(8,128)(2,1)}) %all-reduce.3.cloned.1.call-update) | async-done | bytes 786448 | tf_op jit(solution)/shard_map/psum | solution.py:177
  560.0 596.4 %all-gather.9.cloned.1.call-done = bf16[10,2,1536,512]{3,2,1,0:T(8,128)(2,1)} async-done(((bf16[10,2,192,512]{3,2,1,0:T(8,128)(2,1)}), bf16[10,2,1536,512]{3,2,1,0:T(8,128)(2,1)}) %all-gather.9.cloned.1.call-update) | async-done | bytes 31457296 | tf_op jit(solution)/shard_map/all_gather | solution.py:192
  1156.3 17.0 %fusion.36 = f32[256,10,2,512]{3,0,2,1:T(8,128)} fusion(bf16[10,2,1536,512]{3,2,1,0:T(8,128)(2,1)} %all-gather.9.cloned.1.call-done, bf16[256,1536]{1,0:T(8,128)(2,1)S(1)} %multiply_convert_fusion), kind=kOutput, calls=%fused_computation.67 | convolution fusion | flops 8053063680 | bytes 42729472 | tf_op jit(solution)/shard_map/td,ecdf->tecf/dot_general | solution.py:189
  1173.3 199.8 %all-gather.11.cloned.1.call-done = bf16[10,512,1536]{2,1,0:T(8,128)(2,1)} async-done(((bf16[10,64,1536]{2,1,0:T(8,128)(2,1)}), bf16[10,512,1536]{2,1,0:T(8,128)(2,1)}) %all-gather.11.cloned.1.call-update) | async-done | bytes 15728656 | tf_op jit(solution)/shard_map/all_gather | solution.py:199
  1373.2 13.9 fusion.29
  1387.1 33.0 %all-reduce.5.cloned.1.call-done = bf16[256,1536]{1,0:T(8,128)(2,1)} async-done(((bf16[256,1536]{1,0:T(8,128)(2,1)}), bf16[256,1536]{1,0:T(8,128)(2,1)}) %all-reduce.5.cloned.1.call-update) | async-done | bytes 786448 | tf_op jit(solution)/shard_map/psum | solution.py:202
  (282 shorter events, 147.8 us)
Async XLA Ops:
  7.2 514.8 %copy-start = (bf16[384,1536]{1,0:T(8,128)(2,1)S(1)}, bf16[384,1536]{1,0:T(8,128)(2,1)}, u32[]{:S(2)}) copy-start(bf16[384,1536]{1,0:T(8,128)(2,1)} %param.26) | copy-start | bytes 3538948
  7.2 54.3 %copy-start.14 = (s32[4]{0:T(128)S(1)}, s32[4]{0:T(128)}, u32[]{:S(2)}) copy-start(s32[4]{0:T(128)} %param.25) | copy-start | bytes 52
  7.2 54.3 %all-gather.5.cloned.1.call-start = ((), (), s32[]{:S(2)}) async-start(), calls=%async_computation | async-start | bytes 1769472 | tf_op jit(solution)/shard_map/all_gather | solution.py:117
  13.4 343.9 %all-gather.7.cloned.1.call-start = ((), (), s32[]{:S(2)}) async-start(), calls=%async_computation.1 | async-start | bytes 14155776 | tf_op jit(solution)/shard_map/all_gather | solution.py:15
  178.6 377.9 %all-reduce.3.cloned.1.call-start = ((), (), s32[]{:S(2)}) async-start(), calls=%async_computation.2 | async-start | bytes 1572864 | tf_op jit(solution)/shard_map/psum | solution.py:177
  378.6 9.7 copy-start.3
  378.6 9.7 copy-start.8
  378.6 9.7 copy-start.10
  399.6 9.7 copy-start.3
  399.6 9.7 copy-start.8
  399.6 9.7 copy-start.10
  420.6 9.7 copy-start.3
  420.6 9.7 copy-start.8
  420.6 9.7 copy-start.10
  441.7 9.7 copy-start.3
  441.7 9.7 copy-start.8
  441.7 9.7 copy-start.10
  462.7 9.7 copy-start.3
  462.7 9.7 copy-start.8
  462.7 9.7 copy-start.10
  483.7 9.7 copy-start.3
  483.7 9.7 copy-start.8
  483.7 9.7 copy-start.10
  504.8 9.7 copy-start.8
  504.8 9.7 copy-start.10
  520.8 35.7 %copy-start.5 = (bf16[256,1536]{1,0:T(8,128)(2,1)S(1)}, bf16[256,1536]{1,0:T(8,128)(2,1)}, u32[]{:S(2)}) copy-start(bf16[256,1536]{1,0:T(8,128)(2,1)} %param.18) | copy-start | bytes 2359300
  523.5 35.9 %copy-start.11 = (bf16[1536,40]{0,1:T(8,128)(2,1)S(1)}, bf16[1536,40]{0,1:T(8,128)(2,1)}, u32[]{:S(2)}) copy-start(bf16[1536,40]{0,1:T(8,128)(2,1)} %param.28) | copy-start | bytes 368644
  523.5 36.3 %copy-start.12 = (s32[256,8]{0,1:T(8,128)S(1)}, s32[256,8]{0,1:T(8,128)}, u32[]{:S(2)}) copy-start(s32[256,8]{0,1:T(8,128)} %param.29) | copy-start | bytes 24580
  523.5 632.8 %all-gather.9.cloned.1.call-start = ((), (), s32[]{:S(2)}) async-start(), calls=%async_computation.3 | async-start | bytes 35389440 | tf_op jit(solution)/shard_map/all_gather | solution.py:192
  524.1 849.1 %all-gather.11.cloned.1.call-start = ((), (), s32[]{:S(2)}) async-start(), calls=%async_computation.4 | async-start | bytes 17694720 | tf_op jit(solution)/shard_map/all_gather | solution.py:199
  524.7 895.4 %all-reduce.5.cloned.1.call-start = ((), (), s32[]{:S(2)}) async-start(), calls=%async_computation.5 | async-start | bytes 1572864 | tf_op jit(solution)/shard_map/psum | solution.py:202
  1173.3 246.8 %copy-start.6 = (bf16[256,1536]{1,0:T(8,128)(2,1)S(1)}, bf16[256,1536]{1,0:T(8,128)(2,1)}, u32[]{:S(2)}) copy-start(bf16[256,1536]{1,0:T(8,128)(2,1)} %all-reduce.3.cloned.1.call-done) | copy-start | bytes 2359300
  (29 other events, 70.7 us)
Sparse Core Ops, SparseCore 0:
  13.5 47.9 all-gather.4
  178.7 178.4 all-gather.6
  523.6 32.8 all-reduce.2
  557.9 598.4 all-gather.8
  1158.4 214.7 all-gather.10
  1387.2 32.7 all-reduce.4
where the time goes:
time: 1430 us
  waiting for transfers between devices  1020 us (71%)
  other arithmetic  129 us (9%)
  local copies, waits for them, and re-layouts  112 us (8%)
  matrix products  78.9 us (6%)
  blocking collectives  64 us (4%)
  between operations  14.4 us (1%)
    all_gather x1, waiting for transfers between devices, per_device(): lax.all_gather(w_gate_up, 'seq', axis=2, tiled=True)  596 us
    all_gather x1, waiting for transfers between devices, per_device(): lax.all_gather(w_down, 'seq', axis=1, tiled=True)  200 us
    all_gather x1, waiting for transfers between devices, combined_all(): lax.all_gather(a.astype(kind), axis)  113 us
    add x7, other arithmetic, join_parts(): out_a * factor_a[..., None] + out_b * factor_b[..., None]  67.9 us
    all_gather x2, blocking collectives, combined_all(): lax.all_gather(a.astype(kind), axis)  64 us
    all_gather x1, waiting for transfers between devices, per_device(): lax.all_gather(query_vector.reshape(tok_rows, local_q * HEAD_SIZE), 'seq'...  45.8 us
    dynamic_slice x35, local copies, waits for them, and re-layouts, take(): lax.dynamic_index_in_dim(a, source, 0, False).astype(own.dtype)  44.7 us
    psum x1, waiting for transfers between devices, per_device(): expert_out = lax.psum(moe_part.astype(jnp.bfloat16), 'tp')  33 us
  transfers between devices with their start and end apart: 6, of which 6 were waited for; matrix products, arithmetic and copies ran while one was open for 2% of the time, Pallas kernels for 0%

commit v1 on v0

--- a/solution.py
+++ b/solution.py
@@ -8,6 +8,22 @@
 EPS = 1e-05
 THETA = 10000.0
 NEGATIVE = -1e30
+
+
+def gather_around(x, axis, dim):
+    ways, here, step = (lax.axis_size(axis), lax.axis_index(axis), x.shape[dim])
+    dims = [n * ways if d == dim else n for d, n in enumerate(x.shape)]
+    full = lax.dynamic_update_slice_in_dim(jnp.zeros(dims, x.dtype), x, here * step, axis=dim)
+    going_up = going_down = x
+    for far in range(1, ways // 2 + 1):
+        going_up = lax.ppermute(going_up, axis, [(d, (d + 1) % ways) for d in range(ways)])
+        full = lax.dynamic_update_slice_in_dim(full, going_up, (here - far) % ways * step, axis=dim)
+        if 2 * far < ways:
+            going_down = lax.ppermute(going_down, axis, [(d, (d - 1) % ways) for d in range(ways)])
+            full = lax.dynamic_update_slice_in_dim(
+                full, going_down, (here + far) % ways * step, axis=dim
+            )
+    return full
 
 
 def combined_all(x, axis, join):
@@ -194,10 +210,7 @@
     )
     hidden = (jax.nn.silu(both[:, :, 0]) * both[:, :, 1] * share[:, :, None]).astype(jnp.bfloat16)
     moe_part = jnp.einsum(
-        "tef,efd->td",
-        hidden,
-        lax.all_gather(w_down, "seq", axis=1, tiled=True),
-        preferred_element_type=jnp.float32,
+        "tef,efd->td", hidden, gather_around(w_down, "seq", 1), preferred_element_type=jnp.float32
     )
     expert_out = lax.psum(moe_part.astype(jnp.bfloat16), "tp")
     return (attn_out, expert_out)

time: 1430 us -> 1490 us (1.042)
  waiting for transfers between devices: 1020 us -> 1040 us
  matrix products: 78.9 us -> 96.3 us
  local copies, waits for them, and re-layouts: 112 us -> 128 us
    ppermute x0 -> x7, waiting for transfers between devices: none -> 609 us  [the longest x4 357 us: gather_around(): lax.ppermute(going_up, axis, [(d, (d + 1) % ways) for d in range(ways)])]
    all_gather x1, waiting for transfers between devices: 596 us -> 236 us  [per_device(): lax.all_gather(w_gate_up, 'seq', axis=2, tiled=True)]
    all_gather x1 -> x0, waiting for transfers between devices: 200 us -> none  [per_device(): lax.all_gather(w_down, 'seq', axis=1, tiled=True)]
    psum x1, waiting for transfers between devices: 31.7 us -> 0.01 us  [per_device(): attn = lax.psum(attn_part.astype(jnp.bfloat16), 'tp').astype(jnp.float32)]
    dynamic_update_slice x0 -> x8, local copies, waits for them, and re-layouts: none -> 19.5 us  [the longest x4 10.5 us: gather_around(): lax.dynamic_update_slice_in_dim(full, going_up, (here - far) % ways * ste...]
    dot_general x4, matrix products: 10.5 us -> 27.7 us  [one_request(): jnp.einsum('nhgd,khd->hgnk', query_rows, keys, preferred_element_type=jnp...]
  transfers between devices with their start and end apart: 6 -> 12, of which waited for: 6 -> 9; matrix products, arithmetic and copies ran while one was open for 2% -> 2% of each run, Pallas kernels for 0% -> 0%
where the time goes in v1:
time: 1490 us
  waiting for transfers between devices  1040 us (70%)
  local copies, waits for them, and re-layouts  128 us (9%)
  other arithmetic  121 us (8%)
  matrix products  96.3 us (6%)
  blocking collectives  64 us (4%)
    ppermute x4, waiting for transfers between devices, gather_around(): lax.ppermute(going_up, axis, [(d, (d + 1) % ways) for d in range(ways)])  357 us
    ppermute x3, waiting for transfers between devices, gather_around(): lax.ppermute(going_down, axis, [(d, (d - 1) % ways) for d in range(ways)])  252 us
    all_gather x1, waiting for transfers between devices, per_device(): lax.all_gather(w_gate_up, 'seq', axis=2, tiled=True)  236 us
    all_gather x1, waiting for transfers between devices, combined_all(): lax.all_gather(a.astype(kind), axis)  112 us
    all_gather x2, blocking collectives, combined_all(): lax.all_gather(a.astype(kind), axis)  64 us
    add x7, other arithmetic, join_parts(): out_a * factor_a[..., None] + out_b * factor_b[..., None]  58.5 us
    all_gather x1, waiting for transfers between devices, per_device(): lax.all_gather(query_vector.reshape(tok_rows, local_q * HEAD_SIZE), 'seq'...  45.8 us
    dynamic_slice x35, local copies, waits for them, and re-layouts, take(): lax.dynamic_index_in_dim(a, source, 0, False).astype(own.dtype)  45 us
  transfers between devices with their start and end apart: 12, of which 9 were waited for; matrix products, arithmetic and copies ran while one was open for 2% of the time, Pallas kernels for 0%

profile of v1, /device:TPU:0, one launch (start us, length us, event | category | flops | bytes accessed | tf_op | source)
XLA Modules:
  0.0 1487.4 jit_solution(11154716383032577080)
XLA Ops:
  15.7 45.8 %all-gather.4.cloned.1.call-done = bf16[2048,384]{0,1:T(8,128)(2,1)} async-done(((bf16[256,384]{0,1:T(8,128)(2,1)}), bf16[2048,384]{0,1:T(8,128)(2,1)}) %all-gather.4.cloned.1.call-update) | async-done | bytes 1572880 | tf_op jit(solution)/shard_map/all_gather | solution.py:133
  61.5 128.7 %while.35 = (s32[]{:T(128)}, bf16[4,512,6,64]{1,3,2,0:T(8,128)(2,1)}, bf16[4,512,6]{1,2,0:T(8,128)(2,1)S(1)}, bf16[4,512,6]{1,2,0:T(8,128)(2,1)S(1)}, s32[4]{0:T...) while((s32[]{:T(128)}, ...), condition=%wide.region_5.6_spmd.clone, body=%wide.region_2.5_spmd.clone.sunk | while | flops 1060374528 | bytes 103274912 | solution.py:181
  71.0 6.9 fusion.77
  79.7 8.0 fusion.78
  103.2 6.9 fusion.77
  111.8 8.0 fusion.78
  135.4 6.9 fusion.77
  144.0 8.0 fusion.78
  167.5 6.9 fusion.77
  176.2 8.0 fusion.78
  195.4 31.7 %all_gather.20 = bf16[8,2048,6]{1,2,0:T(8,128)(2,1)S(1)} all-gather(bf16[1,2048,6]{1,2,0:T(8,128)(2,1)S(1)} %bitcast.156), channel_id=1, replica_groups=mesh['seq'=8,'tp'=4] {'seq'}, dimensions={0}, use_global_device_ids=true | all-gather | bytes 221184 | tf_op jit(solution)/shard_map/all_gather | solution.py:31
  228.5 32.3 %all_gather.21 = bf16[8,2048,6]{1,2,0:T(8,128)(2,1)S(1)} all-gather(bf16[1,2048,6]{1,2,0:T(8,128)(2,1)S(1)} %bitcast.157), channel_id=1, replica_groups=mesh['seq'=8,'tp'=4] {'seq'}, dimensions={0}, use_global_device_ids=true | all-gather | bytes 221184 | tf_op jit(solution)/shard_map/all_gather | solution.py:31
  262.1 111.8 %all-gather.6.cloned.1.call-done = bf16[8,2048,6,64]{1,3,2,0:T(8,128)(2,1)} async-done(((bf16[1,2048,6,64]{1,3,2,0:T(8,128)(2,1)}), bf16[8,2048,6,64]{1,3,2,0:T(8,128)(2,1)}) %all-gather.6.cloned.1.call-update) | async-done | bytes 12582928 | tf_op jit(solution)/shard_map/all_gather | solution.py:31
  377.4 6.6 copy.80
  384.0 128.1 %while.34 = (s32[]{:T(128)}, f32[2048,6,64]{2,1,0:T(8,128)}, f32[2048,6]{1,0:T(8,128)}, f32[2048,6]{1,0:T(8,128)}, bf16[8,2048,6]{1,2,0:T(8,128)(2,1)S(1)}, /*in...) while((s32[]{:T(128)}, f32[2048,6,64]{2,1,0:T(8,128)}, ...), condition=%wide.region_7.8_spmd, body=%wide.region_6.7_spmd.sunk | while | flops 3244037 | bytes 21086388 | solution.py:43
  394.0 8.4 fusion.73
  412.3 8.4 fusion.73
  430.5 8.4 fusion.73
  448.8 8.4 fusion.73
  467.1 8.4 fusion.73
  485.4 8.4 fusion.73
  503.7 8.4 fusion.73
  527.5 195.9 %collective-permute-done = bf16[10,64,1536]{2,1,0:T(8,128)(2,1)S(1)} collective-permute-done((bf16[10,64,1536]{2,1,0:T(8,128)(2,1)S(1)}, bf16[10,64,1536]{2,1,0:T(8,128)(2,1)S(1)}, u32[]{:S(2)}, u32[]{:S(2)}) %collective-permute-start) | collective-permute-done | bytes 1966112 | tf_op jit(solution)/shard_map/ppermute | solution.py:19
  725.9 83.1 %collective-permute-done.1 = bf16[10,64,1536]{2,1,0:T(8,128)(2,1)S(1)} collective-permute-done((bf16[10,64,1536]{2,1,0:T(8,128)(2,1)S(1)}, bf16[10,64,1536]{2,1,0:T(8,128)(2,1)S(1)}, u32[]{:S(2)}, u32[]{:S(2)}) %collective-permute-start.1) | collective-permute-done | bytes 1966112 | tf_op jit(solution)/shard_map/ppermute | solution.py:22
  811.1 169.1 %collective-permute-done.3 = bf16[10,64,1536]{2,1,0:T(8,128)(2,1)} collective-permute-done((bf16[10,64,1536]{2,1,0:T(8,128)(2,1)S(1)}, bf16[10,64,1536]{2,1,0:T(8,128)(2,1)}, u32[]{:S(2)}, u32[]{:S(2)}) %collective-permute-start.3) | collective-permute-done | bytes 1966112 | tf_op jit(solution)/shard_map/ppermute | solution.py:22
  980.5 92.4 %collective-permute-done.4 = bf16[10,64,1536]{2,1,0:T(8,128)(2,1)} collective-permute-done((bf16[10,64,1536]{2,1,0:T(8,128)(2,1)}, bf16[10,64,1536]{2,1,0:T(8,128)(2,1)}, u32[]{:S(2)}, u32[]{:S(2)}) %collective-permute-start.4) | collective-permute-done | bytes 1966112 | tf_op jit(solution)/shard_map/ppermute | solution.py:19
  1075.4 6.9 broadcast_in_dim.115
  1099.5 68.9 %collective-permute-done.6 = bf16[10,64,1536]{2,1,0:T(8,128)(2,1)} collective-permute-done((bf16[10,64,1536]{2,1,0:T(8,128)(2,1)}, bf16[10,64,1536]{2,1,0:T(8,128)(2,1)}, u32[]{:S(2)}, u32[]{:S(2)}) %collective-permute-start.6) | collective-permute-done | bytes 1966112 | tf_op jit(solution)/shard_map/ppermute | solution.py:19
  1174.9 235.5 %all-gather.8.cloned.1.call-done = bf16[10,2,1536,512]{3,2,1,0:T(8,128)(2,1)} async-done(((bf16[10,2,192,512]{3,2,1,0:T(8,128)(2,1)}), bf16[10,2,1536,512]{3,2,1,0:T(8,128)(2,1)}) %all-gather.8.cloned.1.call-update) | async-done | bytes 31457296 | tf_op jit(solution)/shard_map/all_gather | solution.py:208
  1410.4 16.5 %fusion.36 = f32[256,10,2,512]{3,0,2,1:T(8,128)} fusion(bf16[10,2,1536,512]{3,2,1,0:T(8,128)(2,1)} %all-gather.8.cloned.1.call-done, bf16[256,1536]{1,0:T(8,128)(2,1)S(1)} %multiply_convert_fusion), kind=kOutput, calls=%fused_computation.67 | convolution fusion | flops 8053063680 | bytes 42729472 | tf_op jit(solution)/shard_map/td,ecdf->tecf/dot_general | solution.py:205
  1427.0 14.0 fusion.29
  1441.0 37.0 %all-reduce.5.cloned.1.call-done = bf16[256,1536]{1,0:T(8,128)(2,1)} async-done(((bf16[256,1536]{1,0:T(8,128)(2,1)}), bf16[256,1536]{1,0:T(8,128)(2,1)}) %all-reduce.5.cloned.1.call-update) | async-done | bytes 786448 | tf_op jit(solution)/shard_map/psum | solution.py:215
  (270 shorter events, 196.6 us)
Async XLA Ops:
  7.2 513.4 %copy-start = (bf16[384,1536]{1,0:T(8,128)(2,1)S(1)}, bf16[384,1536]{1,0:T(8,128)(2,1)}, u32[]{:S(2)}) copy-start(bf16[384,1536]{1,0:T(8,128)(2,1)} %param.26) | copy-start | bytes 3538948
  7.2 54.3 %copy-start.13 = (s32[4]{0:T(128)S(1)}, s32[4]{0:T(128)}, u32[]{:S(2)}) copy-start(s32[4]{0:T(128)} %param.25) | copy-start | bytes 52
  7.2 54.3 %all-gather.4.cloned.1.call-start = ((), (), s32[]{:S(2)}) async-start(), calls=%async_computation | async-start | bytes 1769472 | tf_op jit(solution)/shard_map/all_gather | solution.py:133
  13.4 360.6 %all-gather.6.cloned.1.call-start = ((), (), s32[]{:S(2)}) async-start(), calls=%async_computation.1 | async-start | bytes 14155776 | tf_op jit(solution)/shard_map/all_gather | solution.py:31
  79.6 8.9 slice-start
  79.7 9.2 slice-start.2
  79.7 10.1 slice-start.3
  111.8 9.2 slice-start.2
  111.8 10.1 slice-start.3
  144.0 8.9 slice-start
  144.0 8.9 slice-start.1
  144.0 9.1 slice-start.2
  144.0 10.1 slice-start.3
  176.2 8.9 slice-start
  176.2 9.2 slice-start.2
  176.2 10.1 slice-start.3
  195.3 976.1 %all-reduce.3.cloned.1.call-start = ((), (), s32[]{:S(2)}) async-start(), calls=%async_computation.2 | async-start | bytes 1572864 | tf_op jit(solution)/shard_map/psum | solution.py:193
  518.4 462.1 %copy-start.12 = (bf16[1536]{0:T(1024)(128)(2,1)S(1)}, bf16[1536]{0:T(1024)(128)(2,1)}, u32[]{:S(2)}) copy-start(bf16[1536]{0:T(1024)(128)(2,1)} %param.27) | copy-start | bytes 9220
  522.1 888.4 %all-gather.8.cloned.1.call-start = ((), (), s32[]{:S(2)}) async-start(), calls=%async_computation.3 | async-start | bytes 35389440 | tf_op jit(solution)/shard_map/all_gather | solution.py:208
  522.6 955.3 %all-reduce.5.cloned.1.call-start = ((), (), s32[]{:S(2)}) async-start(), calls=%async_computation.4 | async-start | bytes 1572864 | tf_op jit(solution)/shard_map/psum | solution.py:215
  522.7 200.7 %collective-permute-start = (bf16[10,64,1536]{2,1,0:T(8,128)(2,1)S(1)}, bf16[10,64,1536]{2,1,0:T(8,128)(2,1)S(1)}, u32[]{:S(2)}, u32[]{:S(2)}) collective-permute-start(bf16[10,64,1536]{2,1,0:T(8,128)(2,1)S(1)} %copy-done.5), channel_id=1, source_target_pairs={{0,4},{4,8},{8,12},{12,16},{16,20},{20,24},{24,28},{28,0},{1,5},{5... | collective-permute-start | bytes 5898248 | tf_op jit(solution)/shard_map/ppermute | solution.py:19
  523.3 285.7 %collective-permute-start.1 = (bf16[10,64,1536]{2,1,0:T(8,128)(2,1)S(1)}, bf16[10,64,1536]{2,1,0:T(8,128)(2,1)S(1)}, u32[]{:S(2)}, u32[]{:S(2)}) collective-permute-start(bf16[10,64,1536]{2,1,0:T(8,128)(2,1)S(1)} %copy-done.5), channel_id=1, source_target_pairs={{0,28},{4,0},{8,4},{12,8},{16,12},{20,16},{24,20},{28,24},{1,29},{... | collective-permute-start | bytes 5898248 | tf_op jit(solution)/shard_map/ppermute | solution.py:22
  723.4 85.6 %copy-start.6 = (bf16[10,64,1536]{2,1,0:T(8,128)(2,1)}, bf16[10,64,1536]{2,1,0:T(8,128)(2,1)S(1)}, u32[]{:S(2)}) copy-start(bf16[10,64,1536]{2,1,0:T(8,128)(2,1)S(1)} %collective-permute-done) | copy-start | bytes 5898244
  723.4 87.7 %collective-permute-start.2 = (bf16[10,64,1536]{2,1,0:T(8,128)(2,1)S(1)}, bf16[10,64,1536]{2,1,0:T(8,128)(2,1)}, u32[]{:S(2)}, u32[]{:S(2)}) collective-permute-start(bf16[10,64,1536]{2,1,0:T(8,128)(2,1)S(1)} %collective-permute-done), channel_id=1, source_target_pairs={{0,4},{4,8},{8,12},{12,16},{16,20},{20,24},{24,28},{28,0},{1,5},{5... | collective-permute-start | bytes 5898248 | tf_op jit(solution)/shard_map/ppermute | solution.py:19
  809.0 171.1 %collective-permute-start.3 = (bf16[10,64,1536]{2,1,0:T(8,128)(2,1)S(1)}, bf16[10,64,1536]{2,1,0:T(8,128)(2,1)}, u32[]{:S(2)}, u32[]{:S(2)}) collective-permute-start(bf16[10,64,1536]{2,1,0:T(8,128)(2,1)S(1)} %collective-permute-done.1), channel_id=1, source_target_pairs={{0,28},{4,0},{8,4},{12,8},{16,12},{20,16},{24,20},{28,24},{1,29},{... | collective-permute-start | bytes 5898248 | tf_op jit(solution)/shard_map/ppermute | solution.py:22
  811.1 261.8 %collective-permute-start.4 = (bf16[10,64,1536]{2,1,0:T(8,128)(2,1)}, bf16[10,64,1536]{2,1,0:T(8,128)(2,1)}, u32[]{:S(2)}, u32[]{:S(2)}) collective-permute-start(bf16[10,64,1536]{2,1,0:T(8,128)(2,1)} %collective-permute-done.2), channel_id=1, source_target_pairs={{0,4},{4,8},{8,12},{12,16},{16,20},{20,24},{24,28},{28,0},{1,5},{5... | collective-permute-start | bytes 5898248 | tf_op jit(solution)/shard_map/ppermute | solution.py:19
  980.1 116.4 %collective-permute-start.5 = (bf16[10,64,1536]{2,1,0:T(8,128)(2,1)}, bf16[10,64,1536]{2,1,0:T(8,128)(2,1)}, u32[]{:S(2)}, u32[]{:S(2)}) collective-permute-start(bf16[10,64,1536]{2,1,0:T(8,128)(2,1)} %collective-permute-done.3), channel_id=1, source_target_pairs={{0,28},{4,0},{8,4},{12,8},{16,12},{20,16},{24,20},{28,24},{1,29},{... | collective-permute-start | bytes 5898248 | tf_op jit(solution)/shard_map/ppermute | solution.py:22
  1072.9 95.5 %collective-permute-start.6 = (bf16[10,64,1536]{2,1,0:T(8,128)(2,1)}, bf16[10,64,1536]{2,1,0:T(8,128)(2,1)}, u32[]{:S(2)}, u32[]{:S(2)}) collective-permute-start(bf16[10,64,1536]{2,1,0:T(8,128)(2,1)} %collective-permute-done.4), channel_id=1, source_target_pairs={{0,4},{4,8},{8,12},{12,16},{16,20},{20,24},{24,28},{28,0},{1,5},{5... | collective-permute-start | bytes 5898248 | tf_op jit(solution)/shard_map/ppermute | solution.py:19
  1093.5 77.9 %copy-start.3 = (bf16[256,1536]{1,0:T(8,128)(2,1)S(1)}, bf16[256,1536]{1,0:T(8,128)(2,1)}, u32[]{:S(2)}) copy-start(bf16[256,1536]{1,0:T(8,128)(2,1)} %param.18) | copy-start | bytes 2359300
  1096.5 77.8 %copy-start.10 = (bf16[1536,40]{0,1:T(8,128)(2,1)S(1)}, bf16[1536,40]{0,1:T(8,128)(2,1)}, u32[]{:S(2)}) copy-start(bf16[1536,40]{0,1:T(8,128)(2,1)} %param.28) | copy-start | bytes 368644
  1099.5 75.1 %copy-start.11 = (s32[256,8]{0,1:T(8,128)S(1)}, s32[256,8]{0,1:T(8,128)}, u32[]{:S(2)}) copy-start(s32[256,8]{0,1:T(8,128)} %param.29) | copy-start | bytes 24580
  1427.0 51.0 %copy-start.4 = (bf16[256,1536]{1,0:T(8,128)(2,1)S(1)}, bf16[256,1536]{1,0:T(8,128)(2,1)}, u32[]{:S(2)}) copy-start(bf16[256,1536]{1,0:T(8,128)(2,1)} %all-reduce.3.cloned.1.call-done) | copy-start | bytes 2359300
  (17 other events, 88.3 us)
Sparse Core Ops, SparseCore 0:
  13.5 47.9 all-gather.3
  195.4 178.4 all-gather.5
  522.2 32.8 all-reduce.2
  556.4 853.9 all-gather.7
  1441.1 36.8 all-reduce.4
